TPU v7x, 512 devices: a whole 4x4x16 slice. The times are simulated.
512 devices in a mesh: shell: 128 (over x, z, core), aux: 4 (over y).
Axes of the slice: x: 4, y: 4, z: 16, core: 2. Of those that a mesh axis runs over, the one named last changes fastest.
Arguments:
- integrals: bfloat16 [512, 128, 4, 128], P('shell', None, 'aux'), may hold values from -6 to 6
- pair_list: int32 [512, 3], P('shell'), may hold values from 0 to 511, as said below
- coef: bfloat16 [65536, 1024], P('shell'), may hold values from -0.5 to 0.5
- metric: bfloat16 [4, 4], replicated, may hold values from -3 to 3, as said below
- occ_slot: int32 [128], replicated, may hold values from 0 to 127, each once
Outputs:
- transformed: bfloat16 [1024, 4, 65536], P(('shell', 'aux'))
Inputs may be any that keep to these rules, and one draw needn't show every extreme that they name: `pair_list`: row d * 4 + k holds slot k of index d of shell: block row, block column, live flag. The block column lies in d * 4 to (d + 1) * 4 - 1. On every index live slots come first and at least one is live; some index has all 4 live. `metric`: lower triangular, positive on the diagonal.
All inputs are finite; a program needn't handle non-finite values.
Results may differ from a plain program's by a relative error of at most 0.0054.
Values may be sent and summed in bfloat16 or wider, within the bound.
A program may use at most 64 MiB of HBM per device.

v0:
```python
import jax
import jax.numpy as jnp
from jax import lax
from jax.sharding import PartitionSpec as P

BS = 128


def per_device(integrals, pair_list, coef, metric, occ_slot):
    pairs_dev = pair_list.shape[0]
    rows_local = coef.shape[0]
    occ_count = coef.shape[1]
    blocks_dev = rows_local // BS
    shell_count = lax.axis_size("shell")
    block_count = blocks_dev * shell_count
    slot_count = occ_slot.shape[0]
    aux_dev = integrals.shape[2]
    inverse = (
        jnp.zeros((slot_count,), jnp.int32)
        .at[occ_slot]
        .set(jnp.arange(slot_count, dtype=jnp.int32))
    )
    ordered = jnp.take(
        coef.reshape(rows_local, slot_count, occ_count // slot_count), inverse, axis=1
    )
    ordered = ordered.reshape(rows_local, occ_count)

    def one_slot(item):
        int_block, column_index = item
        start = column_index % blocks_dev * BS
        column = lax.dynamic_slice_in_dim(ordered, start, BS, 0)
        product = lax.dot_general(
            column,
            int_block.reshape(BS, aux_dev * BS),
            (((0,), (0,)), ((), ())),
            preferred_element_type=jnp.float32,
        )
        return product.astype(jnp.bfloat16)

    half_blocks = lax.map(one_slot, (integrals, pair_list[:, 1]))
    half_blocks = half_blocks.reshape(pairs_dev, occ_count, aux_dev, BS)
    listing = lax.all_gather(pair_list, "shell", axis=0, tiled=True)
    targets = jnp.arange(block_count, dtype=jnp.int32)[:, None]
    selector = ((listing[:, 0][None, :] == targets) & (listing[:, 2][None, :] == 1)).astype(
        jnp.bfloat16
    )
    relayed = lax.all_to_all(
        lax.all_to_all(half_blocks, "shell", split_axis=1, concat_axis=0, tiled=True),
        "aux",
        split_axis=1,
        concat_axis=2,
        tiled=True,
    )
    summed = jnp.dot(
        selector, relayed.reshape(relayed.shape[0], -1), preferred_element_type=jnp.float32
    )
    blocks = summed.astype(jnp.bfloat16).reshape((block_count,) + relayed.shape[1:])
    result = jnp.einsum("qp,bipm->iqbm", metric, blocks, preferred_element_type=jnp.float32)
    return result.reshape(result.shape[0], result.shape[1], block_count * BS).astype(jnp.bfloat16)


def solution(mesh):
    placed = (P("shell", None, "aux", None), P("shell", None), P("shell", None), P(), P())
    return jax.shard_map(
        per_device,
        mesh=mesh,
        in_specs=placed,
        out_specs=P(("shell", "aux"), None, None),
        check_vma=False,
    )
```

profile of v0, /device:TPU:1, one launch (start us, length us, event | category | flops | bytes accessed | tf_op | source)
XLA Modules:
  0.0 205.9 jit_solution(11804954031086884912)
XLA Ops:
  0.0 0.0 copy-start
  0.0 0.7 compare_select_fusion.1
  0.7 1.0 scatter_custom_fusion
  1.7 0.0 copy-start.1
  1.7 1.5 copy.23
  3.2 0.1 broadcast_in_dim.32
  3.3 0.1 broadcast_in_dim.33
  3.4 0.0 copy-done.1
  3.4 0.2 slice_reduce_fusion
  3.6 0.6 gather_fusion
  4.3 0.2 bitcast_select_fusion
  4.5 15.1 %while.12 = (s32[]{:T(128)}, bf16[4,1024,128]{2,1,0:T(8,128)(2,1)S(1)}, s32[4]{0:T(128)S(1)}, bf16[512,1024]{0,1:T(8,128)(2,1)S(1)}, bf16[4,128,1,128]{3,1,2,0:T...) while((s32[]{:T(128)}, ...), condition=%wide.region_2.3_spmd, body=%wide.region_1.2_spmd.sunk | while | flops 33685520 | bytes 558360 | solution.py:40
  4.5 0.7 dynamic_slice.31
  7.2 1.0 fusion.22
  8.3 0.7 dynamic_slice.31
  11.0 1.0 fusion.22
  12.0 0.7 dynamic_slice.31
  14.8 1.0 fusion.22
  15.8 0.7 dynamic_slice.31
  18.6 1.0 fusion.22
  19.6 0.8 copy.41
  20.4 74.5 %all_to_all.33 = bf16[4,1024,1,128]{3,0,2,1:T(4,128)(2,1)S(1)} all-to-all(bf16[4,1024,1,128]{3,0,2,1:T(4,128)(2,1)S(1)} %bitcast.50), channel_id=1, replica_groups=mesh['shell'=128,'aux'=4] {'shell'}, dimensions={1} | all-to-all | bytes 2097152 | tf_op jit(solution)/shard_map/all_to_all | solution.py:48
  94.9 0.1 copy.40
  95.1 0.2 copy.27
  95.3 1.1 copy.28
  96.4 4.2 %all-to-all-start.1 = ((bf16[512,8,1,128]{3,0,2,1:T(8,128)(2,1)}), bf16[512,8,1,128]{3,0,2,1:T(8,128)(2,1)S(1)}, u32[]{:S(2)}, u32[]{:S(2)}) async-start(bf16[512,8,1,128]{3,0,2,1:T(8,128)(2,1)} %copy.28), calls=%async_computation.1 | async-start | bytes 2097152 | tf_op jit(solution)/shard_map/all_to_all | solution.py:47
  100.6 100.8 %all-gather = s32[128,4,3]{2,1,0:T(4,128)S(1)} all-gather(s32[1,4,3]{2,1,0:T(4,128)S(1)} %bitcast.55), channel_id=1, replica_groups=mesh['shell'=128,'aux'=4] {'shell'}, dimensions={0}, use_global_device_ids=true | all-gather | bytes 6192 | tf_op jit(solution)/shard_map/all_gather | solution.py:42
  201.4 0.1 fusion.14
  201.5 0.1 copy.34
  201.7 0.1 copy.33
  201.8 0.0 all-to-all-done.1
  201.8 0.5 copy.29
  202.4 0.7 convolution_convert_fusion.2
  203.1 0.8 reshape.43
  203.9 0.0 copy-done
  203.9 0.7 fusion.6
  204.6 1.3 copy.39
  (6 shorter events, 0.1 us)
Async XLA Ops:
  0.0 203.9 %copy-start = (bf16[4,4]{1,0:T(4,128)(2,1)S(1)}, bf16[4,4]{1,0:T(4,128)(2,1)}, u32[]{:S(2)}) copy-start(bf16[4,4]{1,0:T(4,128)(2,1)} %param.10) | copy-start | bytes 100
  1.7 1.7 copy-start.1
  96.4 105.4 %all-to-all-start.1 = ((bf16[512,8,1,128]{3,0,2,1:T(8,128)(2,1)}), bf16[512,8,1,128]{3,0,2,1:T(8,128)(2,1)S(1)}, u32[]{:S(2)}, u32[]{:S(2)}) async-start(bf16[512,8,1,128]{3,0,2,1:T(8,128)(2,1)} %copy.28), calls=%async_computation.1 | async-start | bytes 2097152 | tf_op jit(solution)/shard_map/all_to_all | solution.py:47
where the time goes:
time: 207 us; the launch traced here: 206 us
  blocking collectives  175 us (85%)
  local copies, waits for them, and re-layouts  11.4 us (6%)
  loops' own time  8.45 us (4%)
  matrix products  5.41 us (3%)
  starting transfers between devices  4.18 us (2%)
    all_gather x1, blocking collectives, per_device(): listing = lax.all_gather(pair_list, 'shell', axis=0, tiled=True)  101 us
    all_to_all x1, blocking collectives, per_device(): lax.all_to_all(half_blocks, 'shell', split_axis=1, concat_axis=0, tiled=T...  74.5 us
    another operation x1, loops' own time, per_device(): half_blocks = lax.map(one_slot, (integrals, pair_list[:, 1]))  8.45 us
    all_to_all x1, starting transfers between devices, per_device(): lax.all_to_all(lax.all_to_all(half_blocks, 'shell', split_axis=1, concat_...  4.18 us
  transfers between devices with their start and end apart: 1, of which 0 were waited for; matrix products, arithmetic and copies ran while one was open for 0% of the time, Pallas kernels for 0%

commit v1 on v0

v1 whole, which is shorter than its diff:
```python
import jax
import jax.numpy as jnp
from jax import lax
from jax.experimental import pallas as pl
from jax.experimental.pallas import tpu as pltpu
from jax.sharding import PartitionSpec as P

MESH = pl.DeviceIdType.MESH
BS = 128
OB = 8
NX, NZ, NC, NY = 4, 16, 2, 4
NQ = NX * NC
SLOTS = 4
BLK = SLOTS * BS
ROWS = BLK + 16
CH = 3
CR = ROWS // CH
GROUPS = 9
F32, BF, I32 = jnp.float32, jnp.bfloat16, jnp.int32


def dev(x, z, c, y):
    return ((x * NZ + z) * NC + c, y)


def span(g):
    if g == 0:
        return 0, 1
    if g == 8:
        return 15, 1
    return 2 * g - 1, 2


def move_kernel(
    pair_ref, occ_ref, int_ref, coef_ref, out_ref, rows_ref,
    coef, blk, made, ct, half, relay, tab, tabs,
    s_loc, s_own, ring_s, ring_r, cz_s, cz_r, cy_s, cy_r, x_s, x_r, y_s, y_r, t_s, t_r, xl, yl,
):
    s = lax.axis_index("shell")
    y = lax.axis_index("aux")
    x, z, c = s // (NZ * NC), (s // NC) % NZ, s % NC
    q = x * NC + c
    sg = 1 - 2 * c

    load_coef = pltpu.make_async_copy(coef_ref, coef, s_loc)
    load_coef.start()
    load_int = pltpu.make_async_copy(int_ref, blk.at[0, pl.ds(0, BLK)], s_own)
    load_int.start()

    barrier = pltpu.get_barrier_semaphore()
    peers = [dev(x, (z + d) % NZ, cc, y) for d in range(1, NZ) for cc in range(NC)]
    peers.append(dev(x, z, 1 - c, y))
    peers += [dev((x + d) % NX, z, cc, y) for d in range(1, NX) for cc in range(NC)]
    peers += [dev(x, z, c, (y + d) % NY) for d in range(1, NY)]
    for p in peers:
        pl.semaphore_signal(barrier, inc=1, device_id=p, device_id_type=MESH)

    rid = lax.broadcasted_iota(I32, (16, BS), 0)
    k16 = (rid // 2) % SLOTS
    rv = jnp.zeros((16, BS), I32)
    for k in range(SLOTS):
        rv = jnp.where(k16 == k, pair_ref[k, 0], rv)
    rv = jnp.where(rid < 8, rv // 16, rv % 16)
    blk[0, pl.ds(BLK, 16)] = rv.astype(F32).astype(BF)
    load_int.wait()
    pl.semaphore_wait(barrier, len(peers))

    pending = []

    def remote(src, dst, ss, rs, to):
        m = pltpu.make_async_remote_copy(
            src_ref=src, dst_ref=dst, send_sem=ss, recv_sem=rs, device_id=to, device_id_type=MESH
        )
        m.start()
        pending.append(m)
        return m

    nxt = dev(x, (z + sg + NZ) % NZ, c, y)
    landed = {}

    def ring(j_from, j_to, ch, to):
        part = pl.ds(ch * CR, CR)
        landed[(j_to, ch)] = remote(
            blk.at[j_from, part], blk.at[j_to, part], ring_s.at[j_to, ch], ring_r.at[j_to, ch], to
        )

    for ch in range(CH):
        ring(0, 1, ch, nxt)
        ring(0, 16, ch, dev(x, z, 1 - c, y))

    lane_b = lax.broadcasted_iota(I32, (BS, NZ * NQ * OB), 0)
    col_b = lax.broadcasted_iota(I32, (BS, NZ * NQ * OB), 1)
    expand = jnp.where(col_b // OB == lane_b, 1.0, 0.0).astype(BF)
    occ8 = jnp.broadcast_to(occ_ref[...].astype(F32), (8, BS)).astype(BF)
    occ_col = jnp.dot(occ8, expand, preferred_element_type=F32)[0:1].astype(I32) * OB
    occ_col = occ_col + lax.broadcasted_iota(I32, (1, NZ * NQ * OB), 1) % OB
    load_coef.wait()
    all_coef = coef[...]
    cz = {}

    def forward_ring(d):
        for e in range(2):
            j = 16 if (d == 0 and e == 1) else 2 * d - 1 + e
            if j > 15 and d > 0:
                continue
            for ch in range(CH):
                landed[(j, ch)].wait_recv()
                if d < 7 or (d == 7 and e == 0):
                    ring(j, 2 * d + 1 + e, ch, nxt)

    for uc in range(4):
        rid = lax.broadcasted_iota(I32, (256, BS), 0) + uc * 256
        u, qq, k, o = rid // 64, (rid // 8) % NQ, (rid // 2) % SLOTS, rid % 2
        dist, other = (u + 1) // 2, (u + 1) % 2
        zz = (z + sg * (1 - 2 * other) * dist + NZ) % NZ
        want = (((qq // NC) * NZ + zz) * NC + qq % NC) * OB + y * 2 + o
        pick = jnp.concatenate(
            [
                jnp.where(want == occ_col[:, b * BS : (b + 1) * BS], 1.0, 0.0)
                for b in range(NZ * NQ * OB // BS)
            ],
            axis=1,
        ).astype(BF)
        got = lax.dot_general(pick, all_coef, (((1,), (1,)), ((), ())), preferred_element_type=F32)
        cv = jnp.full((256, BS), -1, I32)
        for kk in range(SLOTS):
            local = jnp.where(pair_ref[kk, 2] == 1, pair_ref[kk, 1] % SLOTS, -1)
            cv = jnp.where(k == kk, local, cv)
        chosen = jnp.zeros((256, BS), F32)
        for b in range(SLOTS):
            chosen = jnp.where(cv == b, got[:, b * BS : (b + 1) * BS], chosen)
        made[pl.ds(4 * uc, 4)] = chosen.astype(BF).reshape(4, 64, BS)
        if uc == 0:
            ct[0, y] = chosen[0:64].astype(BF)
        for uu in range(max(4 * uc, 1), 4 * uc + 4):
            d, e = (uu + 1) // 2, (uu + 1) % 2
            zt = (z + sg * (1 - 2 * e) * d + NZ) % NZ
            ctarget = c if e == 0 else 1 - c
            cz[uu] = remote(
                made.at[uu], ct.at[uu, y], cz_s.at[uu], cz_r.at[uu], dev(x, zt, ctarget, y)
            )
        if uc == 0:
            forward_ring_other(landed, ring, nxt)

    kmask = []
    kid = (lax.broadcasted_iota(I32, (256, BS), 0) // 2) % SLOTS
    for k in range(SLOTS):
        kmask.append(jnp.where(kid == k, 1.0, 0.0).astype(BF))

    cy, xs, ys, xloc, yloc = {}, {}, {}, {}, {}

    def coef_aux(g):
        j0, n = span(g)
        for j in range(j0, j0 + n):
            if j > 0:
                cz[j].wait_recv()
        for dy in range(1, NY):
            part = ct.at[pl.ds(j0, n), y]
            cy[(g, dy)] = remote(
                part, part, cy_s.at[g, dy], cy_r.at[g, dy], dev(x, z, c, (y + dy) % NY)
            )

    def compute(g):
        j0, n = span(g)
        for dy in range(1, NY):
            cy[(g, dy)].wait_recv()
        for j in range(j0, j0 + n):
            lhs = ct[j].reshape(256, BS)
            lhs = jnp.concatenate([lhs * kmask[k] for k in range(SLOTS)], axis=1)
            h = jnp.dot(lhs, blk[j, pl.ds(0, BLK)], preferred_element_type=F32)
            h = h.reshape(NY, NQ, 8, BS)
            for qq in range(NQ):
                half[j, qq] = h[:, qq].astype(BF)
        own = pltpu.make_async_copy(
            half.at[pl.ds(j0, n), q], relay.at[pl.ds(j0, n), :, q], xl.at[g]
        )
        own.start()
        xloc[g] = own
        for dq in range(1, NQ):
            qt = (q + dq) % NQ
            xs[(g, dq)] = remote(
                half.at[pl.ds(j0, n), qt], relay.at[pl.ds(j0, n), :, q],
                x_s.at[g, dq], x_r.at[g, dq], dev(qt // NC, z, qt % NC, y),
            )

    def to_aux(g):
        j0, n = span(g)
        xloc[g].wait()
        for dq in range(1, NQ):
            xs[(g, dq)].wait_recv()
        own = pltpu.make_async_copy(
            relay.at[pl.ds(j0, n), y], out_ref.at[y, pl.ds(j0, n)], yl.at[g]
        )
        own.start()
        yloc[g] = own
        for dy in range(1, NY):
            yt = (y + dy) % NY
            ys[(g, dy)] = remote(
                relay.at[pl.ds(j0, n), yt], out_ref.at[y, pl.ds(j0, n)],
                y_s.at[g, dy], y_r.at[g, dy], dev(x, z, c, yt),
            )

    coef_aux(0)
    coef_aux(1)
    for d in range(1, 9):
        forward_ring(d)
        if d + 1 < GROUPS:
            coef_aux(d + 1)
        compute(d - 1)
        if d >= 3:
            to_aux(d - 3)
    lane = lax.broadcasted_iota(I32, (8, BS), 1)
    table = jnp.zeros((8, BS), F32)
    for j in range(16):
        hi = blk[j, pl.ds(BLK, 16)].astype(F32)
        table = jnp.where(lane == j, hi[0:8] * 16.0 + hi[8:16], table)
    tab[...] = table
    tabs[q] = table
    ts = []
    for dq in range(1, NQ):
        qt = (q + dq) % NQ
        ts.append(
            remote(tab, tabs.at[q], t_s.at[dq], t_r.at[dq], dev(qt // NC, z, qt % NC, y))
        )
    compute(8)
    for g in (6, 7, 8):
        to_aux(g)
    for m in ts:
        m.wait_recv()
    rows_ref[...] = tabs[...]
    for g in range(GROUPS):
        yloc[g].wait()
        for dy in range(1, NY):
            ys[(g, dy)].wait_recv()
    for m in pending:
        m.wait_send()


def forward_ring_other(landed, ring, nxt):
    for ch in range(CH):
        landed[(16, ch)].wait_recv()
        ring(16, 2, ch, nxt)


def sum_kernel(metric_ref, rows_ref, part_ref, out_ref):
    nrho = 1024
    rho = lax.broadcasted_iota(I32, (BS, nrho), 1)
    lane = lax.broadcasted_iota(I32, (BS, nrho), 0)
    by_block = jnp.where(rho // 64 == lane, 1.0, 0.0).astype(BF)
    table = rows_ref[...].reshape(64, BS)
    hi = jnp.floor(table * (1.0 / 16.0))
    lo = table - hi * 16.0
    spread = 16.0 * jnp.dot(hi.astype(BF), by_block, preferred_element_type=F32)
    spread = spread + jnp.dot(lo.astype(BF), by_block, preferred_element_type=F32)
    r64 = lax.broadcasted_iota(I32, (64, nrho), 0)
    c64 = lax.broadcasted_iota(I32, (64, nrho), 1)
    block_row = jnp.sum(jnp.where(c64 % 64 == r64, spread, 0.0), axis=0, keepdims=True)
    o_row = lax.broadcasted_iota(I32, (1, nrho), 1) % 2
    code = block_row.astype(I32) + o_row * 512

    gi = lax.broadcasted_iota(I32, (256, 256), 0)
    gj = lax.broadcasted_iota(I32, (256, 256), 1)
    same = gi // 4 == gj % 64
    mix = jnp.zeros((256, 256), F32)
    for a in range(NY):
        for b in range(NY):
            mix = jnp.where(same & (gi % 4 == a) & (gj // 64 == b), metric_ref[a, b], mix)
    mix = mix.astype(BF)

    parts = jnp.concatenate([part_ref[p].reshape(nrho, BS) for p in range(NY)], axis=1)
    for t in range(4):
        row = lax.broadcasted_iota(I32, (256, nrho), 0) + t * 256
        match = jnp.where(row == code, 1.0, 0.0).astype(BF)
        total = jnp.dot(match, parts, preferred_element_type=F32).astype(BF)
        for b in range(4):
            stack = jnp.concatenate(
                [total[b * 64 : (b + 1) * 64, p * BS : (p + 1) * BS] for p in range(NY)], axis=0
            )
            mixed = jnp.dot(mix, stack, preferred_element_type=F32)
            out_ref[pl.ds((t * 4 + b) * 256, 256)] = mixed.astype(BF)


def per_device(integrals, pair_list, coef, metric, occ_slot):
    dma = pltpu.SemaphoreType.DMA
    any_ = pl.BlockSpec(memory_space=pl.ANY)
    vmem = pl.BlockSpec(memory_space=pltpu.VMEM)
    smem = pl.BlockSpec(memory_space=pltpu.SMEM)
    parts, rows = pl.pallas_call(
        move_kernel,
        name="move",
        out_shape=(
            jax.ShapeDtypeStruct((NY, NZ, NQ, 8, BS), BF),
            jax.ShapeDtypeStruct((NQ, 8, BS), F32),
        ),
        in_specs=[smem, vmem, any_, any_],
        out_specs=(any_, vmem),
        scratch_shapes=[
            pltpu.VMEM((4 * BS, 1024), BF),
            pltpu.VMEM((17, ROWS, BS), BF),
            pltpu.VMEM((NZ, 64, BS), BF),
            pltpu.VMEM((NZ, NY, 64, BS), BF),
            pltpu.VMEM((NZ, NQ, NY, 8, BS), BF),
            pltpu.VMEM((NZ, NY, NQ, 8, BS), BF),
            pltpu.VMEM((8, BS), F32),
            pltpu.VMEM((NQ, 8, BS), F32),
            dma,
            dma,
            dma((17, CH)),
            dma((17, CH)),
            dma((NZ,)),
            dma((NZ,)),
            dma((GROUPS, NY)),
            dma((GROUPS, NY)),
            dma((GROUPS, NQ)),
            dma((GROUPS, NQ)),
            dma((GROUPS, NY)),
            dma((GROUPS, NY)),
            dma((NQ,)),
            dma((NQ,)),
            dma((GROUPS,)),
            dma((GROUPS,)),
        ],
        compiler_params=pltpu.CompilerParams(
            collective_id=0, has_side_effects=True, vmem_limit_bytes=40 << 20
        ),
    )(pair_list, occ_slot.reshape(1, BS), integrals.reshape(BLK, BS), coef)
    out = pl.pallas_call(
        sum_kernel,
        name="sums",
        out_shape=jax.ShapeDtypeStruct((4096, BS), BF),
        in_specs=[smem, vmem, vmem],
        out_specs=vmem,
        compiler_params=pltpu.CompilerParams(vmem_limit_bytes=40 << 20),
    )(metric.astype(F32), rows, parts)
    return out.reshape(2, 512, NY, BS).transpose(0, 2, 1, 3).reshape(2, NY, 512 * BS)


def solution(mesh):
    placed = (P("shell", None, "aux", None), P("shell", None), P("shell", None), P(), P())
    return jax.shard_map(
        per_device,
        mesh=mesh,
        in_specs=placed,
        out_specs=P(("shell", "aux"), None, None),
        check_vma=False,
    )
```

time: 207 us -> 75.6 us (0.37)
  blocking collectives: 175 us -> 0 us
  Pallas kernels: 0 us -> 71.9 us
  loops' own time: 8.45 us -> 0 us
  local copies, waits for them, and re-layouts: 11.4 us -> 3.46 us
  matrix products: 5.41 us -> 0 us
  starting transfers between devices: 4.18 us -> 0 us
    all_gather x1 -> x0, blocking collectives: 101 us -> none  [per_device(): listing = lax.all_gather(pair_list, 'shell', axis=0, tiled=True)]
    all_to_all x1 -> x0, blocking collectives: 74.5 us -> none  [per_device(): lax.all_to_all(half_blocks, 'shell', split_axis=1, concat_axis=0, tiled=T...]
    pallas_call x0 -> x2, Pallas kernels: none -> 71.9 us  [the longest x1 67.8 us: per_device(): pl.pallas_call(move_kernel, name='move', out_shape=(jax.ShapeDtypeStruct(...]
    another operation x1 -> x0, loops' own time: 8.45 us -> none  [per_device(): half_blocks = lax.map(one_slot, (integrals, pair_list[:, 1]))]
    dot_general x6 -> x0, matrix products: 5.41 us -> none  [the longest x4 3.97 us: one_slot(): lax.dot_general(column, int_block.reshape(BS, aux_dev * BS), (((0,), (0,)...]
    all_to_all x1 -> x0, starting transfers between devices: 4.18 us -> none  [per_device(): lax.all_to_all(lax.all_to_all(half_blocks, 'shell', split_axis=1, concat_...]
    dynamic_slice x4 -> x0, local copies, waits for them, and re-layouts: 2.67 us -> none  [per_device(): half_blocks = lax.map(one_slot, (integrals, pair_list[:, 1]))]
  transfers between devices with their start and end apart: 1 -> 0, of which waited for: 0 -> 0; matrix products, arithmetic and copies ran while one was open for 0% -> 0% of each run, Pallas kernels for 0% -> 0%
where the time goes in v1:
time: 75.6 us; the launch traced here: 75.4 us
  Pallas kernels  71.9 us (95%)
  local copies, waits for them, and re-layouts  3.46 us (5%)
    pallas_call x1, Pallas kernels, per_device(): pl.pallas_call(move_kernel, name='move', out_shape=(jax.ShapeDtypeStruct(...  67.8 us
    pallas_call x1, Pallas kernels, per_device(): pl.pallas_call(sum_kernel, name='sums', out_shape=jax.ShapeDtypeStruct((4...  4.13 us
    unnamed x10, local copies, waits for them, and re-layouts  3.46 us

profile of v1, /device:TPU:1, one launch (start us, length us, event | category | flops | bytes accessed | tf_op | source)
XLA Modules:
  0.0 75.4 jit_solution(6302901694027394456)
XLA Ops:
  0.0 0.0 copy-start.4
  0.0 0.0 copy-start.2
  0.0 0.7 copy-done.4
  0.7 0.0 copy-start.3
  0.7 0.0 copy-done.2
  0.7 0.6 copy-done.3
  1.3 0.0 copy-start
  1.3 1.2 %copy-done = bf16[512,1024]{1,0:T(8,128)(2,1)S(1)} copy-done((bf16[512,1024]{1,0:T(8,128)(2,1)S(1)}, bf16[512,1024]{1,0:T(8,128)(2,1)}, u32[]{:S(2)}) %copy-start) | copy-done | bytes 1048600
  2.6 0.0 copy-start.1
  2.6 0.9 %copy-done.1 = bf16[4,128,1,128]{3,1,2,0:T(8,128)(2,1)S(1)} copy-done((bf16[4,128,1,128]{3,1,2,0:T(8,128)(2,1)S(1)}, bf16[4,128,1,128]{3,1,2,0:T(8,128)(2,1)}, u32[]{:S(2)}) %copy-start.1) | copy-done | bytes 131096
  3.5 67.8 %move.1 = (bf16[4,16,8,8,128]{4,3,2,1,0:T(8,128)(2,1)S(1)}, f32[8,8,128]{2,1,0:T(8,128)S(1)}) custom-call(s32[4,3]{1,0:T(4,128)S(1)} %copy-done.2, s32[1,128]{1,0:T(1,128)S(1)} %bitcast.8, bf16[512,128]{1,0:T(8,128)(2,1)S(1)} %bitcast.7, bf16[512,1024]{1,0:T(8,128)(2,1)S(1)} %copy-done), custom_call_target="tpu_custom_call" | custom-call | tf_op jit(solution)/shard_map/move/pallas_call | solution.py:288
  71.2 4.1 %sums.1 = bf16[4096,128]{1,0:T(8,128)(2,1)} custom-call(f32[4,4]{1,0:T(4,128)S(1)} %convert_element_type.3.metric_ref, f32[8,8,128]{2,1,0:T(8,128)S(1)} %get-tuple-element.7.rows_ref, bf16[4,16,8,8,128]{4,3,2,1,0:T(8,128)(2,1)S(1)} %get-tuple-element.8.part_ref), custom_call_target="tpu_custom_call" | custom-call | tf_op jit(solution)/shard_map/sums/pallas_call | solution.py:327
  (1 shorter events, 0.0 us)
Async XLA Ops:
  0.0 0.7 copy-start.4
  0.0 0.7 copy-start.2
  0.7 0.7 copy-start.3
  1.3 1.2 %copy-start = (bf16[512,1024]{1,0:T(8,128)(2,1)S(1)}, bf16[512,1024]{1,0:T(8,128)(2,1)}, u32[]{:S(2)}) copy-start(bf16[512,1024]{1,0:T(8,128)(2,1)} %coef_ref.1) | copy-start | bytes 3145732
  2.6 0.9 %copy-start.1 = (bf16[4,128,1,128]{3,1,2,0:T(8,128)(2,1)S(1)}, bf16[4,128,1,128]{3,1,2,0:T(8,128)(2,1)}, u32[]{:S(2)}) copy-start(bf16[4,128,1,128]{3,1,2,0:T(8,128)(2,1)} %param.5) | copy-start | bytes 393220

commit v2 on v1

v2 whole, which is shorter than its diff:
```python
import jax
import jax.numpy as jnp
from jax import lax
from jax.experimental import pallas as pl
from jax.experimental.pallas import tpu as pltpu
from jax.sharding import PartitionSpec as P

MESH = pl.DeviceIdType.MESH
BS = 128
OB = 8
NX, NZ, NC, NY = 4, 16, 2, 4
NQ = NX * NC
SLOTS = 4
BLK = SLOTS * BS
ROWS = BLK + 16
CUTS = ((0, 256), (256, ROWS - 256))
SPANS = ((0, 3), (3, 2), (5, 2), (7, 2), (9, 2), (11, 2), (13, 2), (15, 1))
GROUPS = len(SPANS)
F32, BF, I32 = jnp.float32, jnp.bfloat16, jnp.int32


def dev(x, z, c, y):
    return ((x * NZ + z) * NC + c, y)


def move_kernel(
    pair_hbm, occ_hbm, int_ref, coef_ref, sums_ref,
    pair_ref, occ_ref, coef, blk, made, ct, half, relay, parts, total, tab, tabs,
    loc, ring_s, ring_r, cz_s, cz_r, cy_s, cy_r, x_s, x_r, y_s, y_r, t_s, t_r, xl, yl, met,
):
    s = lax.axis_index("shell")
    y = lax.axis_index("aux")
    x, z, c = s // (NZ * NC), (s // NC) % NZ, s % NC
    q = x * NC + c
    sg = 1 - 2 * c

    loads = [
        pltpu.make_async_copy(pair_hbm, pair_ref, loc.at[0]),
        pltpu.make_async_copy(int_ref, blk.at[0, pl.ds(0, BLK)], loc.at[1]),
        pltpu.make_async_copy(occ_hbm, occ_ref, loc.at[2]),
        pltpu.make_async_copy(coef_ref, coef, loc.at[3]),
    ]
    for m in loads:
        m.start()

    barrier = pltpu.get_barrier_semaphore()
    near = [dev(x, (z + 1) % NZ, c, y), dev(x, (z + NZ - 1) % NZ, c, y), dev(x, z, 1 - c, y)]
    peers = list(near)
    peers += [dev((x + d) % NX, z, cc, y) for d in range(1, NX) for cc in range(NC)]
    peers += [dev(x, z, c, (y + d) % NY) for d in range(1, NY)]
    for p in peers:
        pl.semaphore_signal(barrier, inc=1, device_id=p, device_id_type=MESH)

    loads[0].wait()
    rid = lax.broadcasted_iota(I32, (16, BS), 0)
    k16 = (rid // 2) % SLOTS
    rv = jnp.zeros((16, BS), I32)
    for k in range(SLOTS):
        rv = jnp.where(k16 == k, pair_ref[k, 0], rv)
    rv = jnp.where(rid < 8, rv // 16, rv % 16)
    blk[0, pl.ds(BLK, 16)] = rv.astype(F32).astype(BF)
    loads[1].wait()
    pl.semaphore_wait(barrier, len(peers))

    def greet(i, to):
        for p in to:
            pl.semaphore_signal(met.at[i], inc=1, device_id=p, device_id_type=MESH)

    def meet(i, n):
        pl.semaphore_wait(met.at[i], n)

    def apart(d):
        return [dev(x, (z + d) % NZ, c, y), dev(x, (z + NZ - d) % NZ, c, y)]

    pending = []

    def remote(src, dst, ss, rs, to):
        m = pltpu.make_async_remote_copy(
            src_ref=src, dst_ref=dst, send_sem=ss, recv_sem=rs, device_id=to, device_id_type=MESH
        )
        m.start()
        pending.append(m)
        return m

    def drain(keep):
        while len(pending) > keep:
            pending.pop(0).wait_send()

    nxt = dev(x, (z + sg + NZ) % NZ, c, y)
    landed = {}

    def ring(j_from, j_to, to):
        for ch, (r0, n) in enumerate(CUTS):
            if (j_from, ch) in landed:
                landed[(j_from, ch)].wait_recv()
            part = pl.ds(r0, n)
            landed[(j_to, ch)] = remote(
                blk.at[j_from, part], blk.at[j_to, part], ring_s.at[j_to, ch], ring_r.at[j_to, ch], to
            )

    def arrive(j):
        for ch in range(len(CUTS)):
            landed[(j, ch)].wait_recv()

    def step(d, e):
        j = 2 * d - 1 + e
        if d < 7 or (d == 7 and e == 0):
            ring(j, j + 2, nxt)
        else:
            arrive(j)

    ring(0, 1, nxt)
    ring(0, 16, dev(x, z, 1 - c, y))
    greet(0, near)

    ncol = NZ * NQ * OB
    loads[2].wait()
    lane_b = lax.broadcasted_iota(I32, (BS, ncol), 0)
    col_b = lax.broadcasted_iota(I32, (BS, ncol), 1)
    expand = jnp.where(col_b // OB == lane_b, 1.0, 0.0).astype(BF)
    occ8 = jnp.broadcast_to(occ_ref[...].astype(F32), (8, BS)).astype(BF)
    occ_col = jnp.dot(occ8, expand, preferred_element_type=F32)[0:1].astype(I32) * OB
    occ_col = occ_col + lax.broadcasted_iota(I32, (1, ncol), 1) % OB
    loads[3].wait()
    cz = {}

    def coef_chunk(uc):
        rid = lax.broadcasted_iota(I32, (256, BS), 0) + uc * 256
        u, qq, k, o = rid // 64, (rid // 8) % NQ, (rid // 2) % SLOTS, rid % 2
        dist, other = (u + 1) // 2, (u + 1) % 2
        zz = (z + sg * (1 - 2 * other) * dist + NZ) % NZ
        want = (((qq // NC) * NZ + zz) * NC + qq % NC) * OB + y * 2 + o
        pick = jnp.concatenate(
            [
                jnp.where(want == occ_col[:, b * BS : (b + 1) * BS], 1.0, 0.0)
                for b in range(ncol // BS)
            ],
            axis=1,
        ).astype(BF)
        got = lax.dot_general(
            pick, coef[...], (((1,), (1,)), ((), ())), preferred_element_type=F32
        )
        cv = jnp.full((256, BS), -1, I32)
        for kk in range(SLOTS):
            local = jnp.where(pair_ref[kk, 2] == 1, pair_ref[kk, 1] % SLOTS, -1)
            cv = jnp.where(k == kk, local, cv)
        chosen = jnp.zeros((256, BS), F32)
        for b in range(SLOTS):
            chosen = jnp.where(cv == b, got[:, b * BS : (b + 1) * BS], chosen)
        made[pl.ds(4 * uc, 4)] = chosen.astype(BF).reshape(4, 64, BS)
        if uc == 0:
            ct[0, y] = chosen[0:64].astype(BF)

    def coef_out(*dist):
        for d in dist:
            for e in range(2 if d < 8 else 1):
                u = 2 * d - 1 + e
                zt = (z + sg * (1 - 2 * e) * d + NZ) % NZ
                ctarget = c if e == 0 else 1 - c
                cz[u] = remote(
                    made.at[u], ct.at[u, y], cz_s.at[u], cz_r.at[u], dev(x, zt, ctarget, y)
                )

    coef_chunk(0)
    meet(0, 3)
    greet(1, apart(2))
    ring(16, 2, nxt)
    coef_out(1)
    coef_chunk(1)
    meet(1, 2)
    greet(2, apart(4))
    coef_out(2, 3)
    coef_chunk(2)
    step(1, 0)
    meet(2, 2)
    coef_out(4, 5)
    coef_chunk(3)
    step(1, 1)
    coef_out(6, 7, 8)

    kid = (lax.broadcasted_iota(I32, (256, BS), 0) // 2) % SLOTS
    kmask = [jnp.where(kid == k, 1.0, 0.0).astype(BF) for k in range(SLOTS)]
    cy, xs, ys, xloc, yloc = {}, {}, {}, {}, {}

    def coef_aux(g):
        j0, n = SPANS[g]
        for j in range(j0, j0 + n):
            if j > 0:
                cz[j].wait_recv()
        for dy in range(1, NY):
            part = ct.at[pl.ds(j0, n), y]
            cy[(g, dy)] = remote(
                part, part, cy_s.at[g, dy], cy_r.at[g, dy], dev(x, z, c, (y + dy) % NY)
            )

    def compute(g):
        j0, n = SPANS[g]
        for dy in range(1, NY):
            cy[(g, dy)].wait_recv()
        for j in range(j0, j0 + n):
            lhs = ct[j].reshape(256, BS)
            lhs = jnp.concatenate([lhs * kmask[k] for k in range(SLOTS)], axis=1)
            h = jnp.dot(lhs, blk[j, pl.ds(0, BLK)], preferred_element_type=F32)
            h = h.reshape(NY, NQ, 8, BS)
            for qq in range(NQ):
                half[j, qq] = h[:, qq].astype(BF)
        here = pl.ds(j0, n)
        xloc[g] = pltpu.make_async_copy(half.at[here, q], relay.at[here, :, q], xl.at[g])
        xloc[g].start()
        for dq in range(1, NQ):
            qt = (q + dq) % NQ
            xs[(g, dq)] = remote(
                half.at[here, qt], relay.at[here, :, q],
                x_s.at[g, dq], x_r.at[g, dq], dev(qt // NC, z, qt % NC, y),
            )

    def to_aux(g):
        j0, n = SPANS[g]
        here = pl.ds(j0, n)
        xloc[g].wait()
        for dq in range(1, NQ):
            xs[(g, dq)].wait_recv()
        yloc[g] = pltpu.make_async_copy(relay.at[here, y], parts.at[y, here], yl.at[g])
        yloc[g].start()
        for dy in range(1, NY):
            yt = (y + dy) % NY
            ys[(g, dy)] = remote(
                relay.at[here, yt], parts.at[y, here],
                y_s.at[g, dy], y_r.at[g, dy], dev(x, z, c, yt),
            )

    def arrived(g):
        yloc[g].wait()
        for dy in range(1, NY):
            ys[(g, dy)].wait_recv()

    lane8 = lax.broadcasted_iota(I32, (8, BS), 1)
    tabled = {}

    def rows_out(i, j0, n):
        table = jnp.zeros((8, BS), F32)
        for j in range(j0, j0 + n):
            ids = blk[j, pl.ds(BLK, 16)].astype(F32)
            table = jnp.where(lane8 == j, ids[0:8] * 16.0 + ids[8:16], table)
        tab[i] = table
        tabs[i, q] = table
        for dq in range(1, NQ):
            qt = (q + dq) % NQ
            tabled[(i, dq)] = remote(
                tab.at[i], tabs.at[i, q], t_s.at[i, dq], t_r.at[i, dq], dev(qt // NC, z, qt % NC, y)
            )

    lane1 = lax.broadcasted_iota(I32, (1, BS), 1)
    code_of = {}

    def codes(i, j0, n):
        for dq in range(1, NQ):
            tabled[(i, dq)].wait_recv()
        turned = jnp.transpose(jnp.concatenate([tabs[i].reshape(64, BS)] * 2, axis=0))
        for j in range(j0, j0 + n, 2):
            both = jnp.where(lane1 < 64, turned[j : j + 1], turned[j + 1 : j + 2])
            code_of[j] = both.astype(I32) + (lane1 % 2) * 512

    def add_up(j0, n, first, last):
        code = [code_of[j] for j in range(j0, j0 + n, 2)]
        terms = jnp.concatenate(
            [parts[p, pl.ds(j0, n)].reshape(n * 64, BS) for p in range(NY)], axis=1
        )
        for t in range(4):
            row = lax.broadcasted_iota(I32, (256, BS), 0) + t * 256
            match = jnp.concatenate([jnp.where(row == v, 1.0, 0.0) for v in code], axis=1)
            got = jnp.dot(match.astype(BF), terms, preferred_element_type=F32)
            here = pl.ds(t * 256, 256)
            if first:
                total[here] = got
            elif last:
                sums_ref[here] = (total[here] + got).astype(BF)
            else:
                total[here] = total[here] + got

    coef_aux(0)
    step(2, 0)
    step(2, 1)
    coef_aux(1)
    compute(0)
    step(3, 0)
    step(3, 1)
    coef_aux(2)
    compute(1)
    to_aux(0)
    drain(24)
    step(4, 0)
    step(4, 1)
    coef_aux(3)
    compute(2)
    to_aux(1)
    drain(24)
    step(5, 0)
    step(5, 1)
    coef_aux(4)
    compute(3)
    to_aux(2)
    arrived(0)
    step(6, 0)
    step(6, 1)
    coef_aux(5)
    coef_aux(6)
    coef_aux(7)
    compute(4)
    rows_out(0, 0, 12)
    to_aux(3)
    step(7, 0)
    step(7, 1)
    compute(5)
    compute(6)
    to_aux(4)
    step(8, 0)
    compute(7)
    rows_out(1, 12, 4)
    to_aux(5)
    arrived(1)
    arrived(2)
    codes(0, 0, 12)
    add_up(0, 6, True, False)
    to_aux(6)
    to_aux(7)
    arrived(3)
    arrived(4)
    arrived(5)
    add_up(6, 6, False, False)
    codes(1, 12, 4)
    drain(6)
    arrived(6)
    arrived(7)
    add_up(12, 4, False, True)
    drain(0)


def mix_kernel(metric_ref, sums_ref, out_ref, mixed, sems):
    ri = lax.broadcasted_iota(I32, (256, 8), 0)
    ci = lax.broadcasted_iota(I32, (256, 8), 1)
    rows4 = jnp.where(ri % 4 == ci, 1.0, 0.0)[:, 0:4].astype(BF)
    rj = lax.broadcasted_iota(I32, (8, 256), 0)
    cj = lax.broadcasted_iota(I32, (8, 256), 1)
    cols4 = jnp.where(cj // 64 == rj, 1.0, 0.0)[0:4].astype(BF)
    spread = jnp.dot(rows4, metric_ref[...], preferred_element_type=F32).astype(BF)
    spread = jnp.dot(spread, cols4, preferred_element_type=F32)
    gi = lax.broadcasted_iota(I32, (256, 256), 0)
    gj = lax.broadcasted_iota(I32, (256, 256), 1)
    mix = jnp.where(gi // 4 == gj % 64, spread, 0.0).astype(BF)
    copies = []
    for t in range(4):
        for b in range(4 * t, 4 * t + 4):
            stack = jnp.concatenate(
                [sums_ref[pl.ds(b * 64, 64), p * BS : (p + 1) * BS] for p in range(NY)], axis=0
            )
            mixed[pl.ds(b * 256, 256)] = jnp.dot(mix, stack, preferred_element_type=F32).astype(BF)
        here = pl.ds(t * 1024, 1024)
        copies.append(pltpu.make_async_copy(mixed.at[here], out_ref.at[here], sems.at[t]))
        copies[-1].start()
    for m in copies:
        m.wait()


def per_device(integrals, pair_list, coef, metric, occ_slot):
    dma = pltpu.SemaphoreType.DMA
    hbm = pl.BlockSpec(memory_space=pltpu.HBM)
    vmem = pl.BlockSpec(memory_space=pltpu.VMEM)
    operands = (pair_list, occ_slot.reshape(1, BS), integrals.reshape(BLK, BS), coef)
    sums = pl.pallas_call(
        move_kernel,
        name="move",
        out_shape=jax.ShapeDtypeStruct((1024, NY * BS), BF),
        in_specs=[hbm, hbm, hbm, hbm],
        out_specs=vmem,
        scratch_shapes=[
            pltpu.SMEM((SLOTS, 3), I32),
            pltpu.VMEM((1, BS), I32),
            pltpu.VMEM((4 * BS, 1024), BF),
            pltpu.VMEM((17, ROWS, BS), BF),
            pltpu.VMEM((NZ, 64, BS), BF),
            pltpu.VMEM((NZ, NY, 64, BS), BF),
            pltpu.VMEM((NZ, NQ, NY, 8, BS), BF),
            pltpu.VMEM((NZ, NY, NQ, 8, BS), BF),
            pltpu.VMEM((NY, NZ, NQ, 8, BS), BF),
            pltpu.VMEM((1024, NY * BS), F32),
            pltpu.VMEM((2, 8, BS), F32),
            pltpu.VMEM((2, NQ, 8, BS), F32),
            dma((4,)),
            dma((17, len(CUTS))),
            dma((17, len(CUTS))),
            dma((NZ,)),
            dma((NZ,)),
            dma((GROUPS, NY)),
            dma((GROUPS, NY)),
            dma((GROUPS, NQ)),
            dma((GROUPS, NQ)),
            dma((GROUPS, NY)),
            dma((GROUPS, NY)),
            dma((2, NQ)),
            dma((2, NQ)),
            dma((GROUPS,)),
            dma((GROUPS,)),
            pltpu.SemaphoreType.REGULAR((3,)),
        ],
        compiler_params=pltpu.CompilerParams(
            collective_id=0, has_side_effects=True, vmem_limit_bytes=40 << 20
        ),
    )(*(pltpu.with_memory_space_constraint(a, pltpu.HBM) for a in operands))
    out = pl.pallas_call(
        mix_kernel,
        name="mix",
        out_shape=jax.ShapeDtypeStruct((4096, BS), BF),
        in_specs=[vmem, vmem],
        out_specs=hbm,
        scratch_shapes=[pltpu.VMEM((4096, BS), BF), dma((4,))],
        compiler_params=pltpu.CompilerParams(vmem_limit_bytes=40 << 20),
    )(metric, sums)
    return out.reshape(2, 512, NY, BS).transpose(0, 2, 1, 3).reshape(2, NY, 512 * BS)


def solution(mesh):
    placed = (P("shell", None, "aux", None), P("shell", None), P("shell", None), P(), P())
    return jax.shard_map(
        per_device,
        mesh=mesh,
        in_specs=placed,
        out_specs=P(("shell", "aux"), None, None),
        check_vma=False,
    )
```

time: 75.6 us -> 68.6 us (0.907)
  local copies, waits for them, and re-layouts: 3.46 us -> 0.01 us
  Pallas kernels: 71.9 us -> 68.5 us
    unnamed x10 -> x2, local copies, waits for them, and re-layouts: 3.46 us -> 0.01 us
    pallas_call x2, Pallas kernels: 71.9 us -> 68.5 us  [the longest x1 66.8 us: per_device(): pl.pallas_call(move_kernel, name='move', out_shape=jax.ShapeDtypeStruct((...]
where the time goes in v2:
time: 68.6 us; the launch traced here: 68.5 us
  Pallas kernels  68.5 us (100%)
    pallas_call x1, Pallas kernels, per_device(): pl.pallas_call(move_kernel, name='move', out_shape=jax.ShapeDtypeStruct((...  66.8 us
    pallas_call x1, Pallas kernels, per_device(): pl.pallas_call(mix_kernel, name='mix', out_shape=jax.ShapeDtypeStruct((40...  1.67 us

profile of v2, /device:TPU:1, one launch (start us, length us, event | category | flops | bytes accessed | tf_op | source)
XLA Modules:
  0.0 68.5 jit_solution(6594411505601389881)
XLA Ops:
  0.0 0.0 copy-start
  0.0 66.8 %move.1.sums_ref = bf16[1024,512]{1,0:T(8,128)(2,1)S(1)} custom-call(s32[4,3]{1,0:T(4,128)} %pair_hbm.1, s32[1,128]{1,0:T(1,128)} %bitcast.8, bf16[512,128]{1,0:T(8,128)(2,1)} %bitcast.7, bf16[512,1024]{1,0:T(8,128)(2,1)} %coef_ref.1), custom_call_target="tpu_custom_call" | custom-call | tf_op jit(solution)/shard_map/move/pallas_call | solution.py:370
  66.8 0.0 copy-done
  66.8 1.7 %mix.1 = bf16[4096,128]{1,0:T(8,128)(2,1)} custom-call(bf16[4,4]{1,0:T(4,128)(2,1)S(1)} %copy-done, bf16[1024,512]{1,0:T(8,128)(2,1)S(1)} %move.1.sums_ref), custom_call_target="tpu_custom_call" | custom-call | tf_op jit(solution)/shard_map/mix/pallas_call | solution.py:410
Async XLA Ops:
  0.0 66.8 %copy-start = (bf16[4,4]{1,0:T(4,128)(2,1)S(1)}, bf16[4,4]{1,0:T(4,128)(2,1)}, u32[]{:S(2)}) copy-start(bf16[4,4]{1,0:T(4,128)(2,1)} %metric_ref.1) | copy-start | bytes 100

commit v3 on v2

--- a/solution.py
+++ b/solution.py
@@ -25,7 +25,7 @@
 
 def move_kernel(
     pair_hbm, occ_hbm, int_ref, coef_ref, sums_ref,
-    pair_ref, occ_ref, coef, blk, made, ct, half, relay, parts, total, tab, tabs,
+    pair_ref, occ_ref, coef, blk, made, ct, half, relay, parts, total, tab, tabs, picked,
     loc, ring_s, ring_r, cz_s, cz_r, cy_s, cy_r, x_s, x_r, y_s, y_r, t_s, t_r, xl, yl, met,
 ):
     s = lax.axis_index("shell")
@@ -59,77 +59,21 @@
         rv = jnp.where(k16 == k, pair_ref[k, 0], rv)
     rv = jnp.where(rid < 8, rv // 16, rv % 16)
     blk[0, pl.ds(BLK, 16)] = rv.astype(F32).astype(BF)
-    loads[1].wait()
-    pl.semaphore_wait(barrier, len(peers))
-
-    def greet(i, to):
-        for p in to:
-            pl.semaphore_signal(met.at[i], inc=1, device_id=p, device_id_type=MESH)
-
-    def meet(i, n):
-        pl.semaphore_wait(met.at[i], n)
-
-    def apart(d):
-        return [dev(x, (z + d) % NZ, c, y), dev(x, (z + NZ - d) % NZ, c, y)]
-
-    pending = []
-
-    def remote(src, dst, ss, rs, to):
-        m = pltpu.make_async_remote_copy(
-            src_ref=src, dst_ref=dst, send_sem=ss, recv_sem=rs, device_id=to, device_id_type=MESH
-        )
-        m.start()
-        pending.append(m)
-        return m
-
-    def drain(keep):
-        while len(pending) > keep:
-            pending.pop(0).wait_send()
-
-    nxt = dev(x, (z + sg + NZ) % NZ, c, y)
-    landed = {}
-
-    def ring(j_from, j_to, to):
-        for ch, (r0, n) in enumerate(CUTS):
-            if (j_from, ch) in landed:
-                landed[(j_from, ch)].wait_recv()
-            part = pl.ds(r0, n)
-            landed[(j_to, ch)] = remote(
-                blk.at[j_from, part], blk.at[j_to, part], ring_s.at[j_to, ch], ring_r.at[j_to, ch], to
-            )
-
-    def arrive(j):
-        for ch in range(len(CUTS)):
-            landed[(j, ch)].wait_recv()
-
-    def step(d, e):
-        j = 2 * d - 1 + e
-        if d < 7 or (d == 7 and e == 0):
-            ring(j, j + 2, nxt)
-        else:
-            arrive(j)
-
-    ring(0, 1, nxt)
-    ring(0, 16, dev(x, z, 1 - c, y))
-    greet(0, near)
-
     ncol = NZ * NQ * OB
     loads[2].wait()
     lane_b = lax.broadcasted_iota(I32, (BS, ncol), 0)
     col_b = lax.broadcasted_iota(I32, (BS, ncol), 1)
-    expand = jnp.where(col_b // OB == lane_b, 1.0, 0.0).astype(BF)
+    expand = jnp.where(col_b >> 3 == lane_b, 1.0, 0.0).astype(BF)
     occ8 = jnp.broadcast_to(occ_ref[...].astype(F32), (8, BS)).astype(BF)
     occ_col = jnp.dot(occ8, expand, preferred_element_type=F32)[0:1].astype(I32) * OB
-    occ_col = occ_col + lax.broadcasted_iota(I32, (1, ncol), 1) % OB
+    occ_col = occ_col + (lax.broadcasted_iota(I32, (1, ncol), 1) & (OB - 1))
     loads[3].wait()
-    cz = {}
-
-    def coef_chunk(uc):
-        rid = lax.broadcasted_iota(I32, (256, BS), 0) + uc * 256
-        u, qq, k, o = rid // 64, (rid // 8) % NQ, (rid // 2) % SLOTS, rid % 2
-        dist, other = (u + 1) // 2, (u + 1) % 2
-        zz = (z + sg * (1 - 2 * other) * dist + NZ) % NZ
-        want = (((qq // NC) * NZ + zz) * NC + qq % NC) * OB + y * 2 + o
+    def coef_pick():
+        rid = lax.broadcasted_iota(I32, (256, BS), 0)
+        u, qq, o = rid >> 4, (rid >> 1) & (NQ - 1), rid & 1
+        dist, other = (u + 1) >> 1, (u + 1) & 1
+        zz = (z + sg * (1 - 2 * other) * dist + NZ) & (NZ - 1)
+        want = (((qq >> 1) * NZ + zz) * NC + (qq & 1)) * OB + y * 2 + o
         pick = jnp.concatenate(
             [
                 jnp.where(want == occ_col[:, b * BS : (b + 1) * BS], 1.0, 0.0)
@@ -140,16 +84,85 @@
         got = lax.dot_general(
             pick, coef[...], (((1,), (1,)), ((), ())), preferred_element_type=F32
         )
-        cv = jnp.full((256, BS), -1, I32)
-        for kk in range(SLOTS):
-            local = jnp.where(pair_ref[kk, 2] == 1, pair_ref[kk, 1] % SLOTS, -1)
-            cv = jnp.where(k == kk, local, cv)
-        chosen = jnp.zeros((256, BS), F32)
-        for b in range(SLOTS):
-            chosen = jnp.where(cv == b, got[:, b * BS : (b + 1) * BS], chosen)
-        made[pl.ds(4 * uc, 4)] = chosen.astype(BF).reshape(4, 64, BS)
+        for k in range(SLOTS):
+            local = jnp.where(pair_ref[k, 2] == 1, pair_ref[k, 1] % SLOTS, -1)
+            chosen = jnp.zeros((256, BS), F32)
+            for b in range(SLOTS):
+                chosen += jnp.where(local == b, 1.0, 0.0) * got[:, b * BS : (b + 1) * BS]
+            picked[k] = chosen.astype(BF)
+
+    pr = lax.broadcasted_iota(I32, (256, 256), 0)
+    pc = lax.broadcasted_iota(I32, (256, 256), 1)
+    order = ((pr >> 1) & 3) * 64 + (pr >> 6) * 16 + ((pr >> 3) & 7) * 2 + (pr & 1)
+    order = jnp.where(order == pc, 1.0, 0.0).astype(BF)
+
+    def coef_chunk(uc):
+        stack = picked[:, pl.ds(64 * uc, 64)].reshape(256, BS)
+        chosen = jnp.dot(order, stack, preferred_element_type=F32).astype(BF)
+        made[pl.ds(4 * uc, 4)] = chosen.reshape(4, 64, BS)
         if uc == 0:
-            ct[0, y] = chosen[0:64].astype(BF)
+            ct[0, y] = chosen[0:64]
+
+    coef_pick()
+    coef_chunk(0)
+    coef_chunk(1)
+    coef_chunk(2)
+    coef_chunk(3)
+    loads[1].wait()
+    pl.semaphore_wait(barrier, len(peers))
+
+    def greet(i, to):
+        for p in to:
+            pl.semaphore_signal(met.at[i], inc=1, device_id=p, device_id_type=MESH)
+
+    def meet(i, n):
+        pl.semaphore_wait(met.at[i], n)
+
+    def apart(d):
+        return [dev(x, (z + d) % NZ, c, y), dev(x, (z + NZ - d) % NZ, c, y)]
+
+    pending = []
+
+    def remote(src, dst, ss, rs, to):
+        m = pltpu.make_async_remote_copy(
+            src_ref=src, dst_ref=dst, send_sem=ss, recv_sem=rs, device_id=to, device_id_type=MESH
+        )
+        m.start()
+        pending.append(m)
+        return m
+
+    def drain(keep):
+        while len(pending) > keep:
+            pending.pop(0).wait_send()
+
+    nxt = dev(x, (z + sg + NZ) % NZ, c, y)
+    landed = {}
+
+    def ring(j_from, j_to, to):
+        for ch, (r0, n) in enumerate(CUTS):
+            if (j_from, ch) in landed:
+                landed[(j_from, ch)].wait_recv()
+            part = pl.ds(r0, n)
+            landed[(j_to, ch)] = remote(
+                blk.at[j_from, part], blk.at[j_to, part], ring_s.at[j_to, ch], ring_r.at[j_to, ch], to
+            )
+
+    def arrive(j):
+        for ch in range(len(CUTS)):
+            landed[(j, ch)].wait_recv()
+
+    def step(d, e):
+        j = 2 * d - 1 + e
+        if d < 7 or (d == 7 and e == 0):
+            ring(j, j + 2, nxt)
+        else:
+            arrive(j)
+
+    ring(0, 1, nxt)
+    ring(0, 16, dev(x, z, 1 - c, y))
+    greet(0, near)
+
+    cz = {}
 
     def coef_out(*dist):
         for d in dist:
@@ -161,22 +174,17 @@
                     made.at[u], ct.at[u, y], cz_s.at[u], cz_r.at[u], dev(x, zt, ctarget, y)
                 )
 
-    coef_chunk(0)
     meet(0, 3)
     greet(1, apart(2))
     ring(16, 2, nxt)
     coef_out(1)
-    coef_chunk(1)
     meet(1, 2)
     greet(2, apart(4))
     coef_out(2, 3)
-    coef_chunk(2)
     step(1, 0)
     meet(2, 2)
+    step(1, 1)
     coef_out(4, 5)
-    coef_chunk(3)
-    step(1, 1)
-    coef_out(6, 7, 8)
 
     kid = (lax.broadcasted_iota(I32, (256, BS), 0) // 2) % SLOTS
     kmask = [jnp.where(kid == k, 1.0, 0.0).astype(BF) for k in range(SLOTS)]
@@ -281,51 +289,54 @@
     coef_aux(0)
     step(2, 0)
     step(2, 1)
+    coef_out(6, 7, 8)
     coef_aux(1)
+    coef_aux(2)
     compute(0)
     step(3, 0)
     step(3, 1)
-    coef_aux(2)
+    coef_aux(3)
     compute(1)
+    compute(2)
     to_aux(0)
-    drain(24)
     step(4, 0)
     step(4, 1)
-    coef_aux(3)
-    compute(2)
+    coef_aux(4)
+    coef_aux(5)
+    compute(3)
     to_aux(1)
-    drain(24)
+    to_aux(2)
+    drain(28)
     step(5, 0)
     step(5, 1)
-    coef_aux(4)
-    compute(3)
-    to_aux(2)
-    arrived(0)
-    step(6, 0)
-    step(6, 1)
-    coef_aux(5)
     coef_aux(6)
     coef_aux(7)
     compute(4)
+    to_aux(3)
+    drain(28)
+    step(6, 0)
+    step(6, 1)
+    compute(5)
+    to_aux(4)
     rows_out(0, 0, 12)
-    to_aux(3)
+    drain(34)
     step(7, 0)
     step(7, 1)
-    compute(5)
     compute(6)
-    to_aux(4)
+    to_aux(5)
+    arrived(0)
+    arrived(1)
+    codes(0, 0, 12)
+    drain(20)
     step(8, 0)
     compute(7)
     rows_out(1, 12, 4)
-    to_aux(5)
-    arrived(1)
+    to_aux(6)
     arrived(2)
-    codes(0, 0, 12)
     add_up(0, 6, True, False)
-    to_aux(6)
-    to_aux(7)
     arrived(3)
     arrived(4)
+    to_aux(7)
     arrived(5)
     add_up(6, 6, False, False)
     codes(1, 12, 4)
@@ -386,6 +397,7 @@
             pltpu.VMEM((1024, NY * BS), F32),
             pltpu.VMEM((2, 8, BS), F32),
             pltpu.VMEM((2, NQ, 8, BS), F32),
+            pltpu.VMEM((SLOTS, 256, BS), BF),
             dma((4,)),
             dma((17, len(CUTS))),
             dma((17, len(CUTS))),

time: 68.6 us -> 65.8 us (0.959)
  Pallas kernels: 68.5 us -> 65.6 us
    pallas_call x1, Pallas kernels: 66.8 us -> 64 us  [per_device(): pl.pallas_call(move_kernel, name='move', out_shape=jax.ShapeDtypeStruct((...]
where the time goes in v3:
time: 65.8 us; the launch traced here: 65.6 us
  Pallas kernels  65.6 us (100%)
    pallas_call x1, Pallas kernels, per_device(): pl.pallas_call(move_kernel, name='move', out_shape=jax.ShapeDtypeStruct((...  64 us
    pallas_call x1, Pallas kernels, per_device(): pl.pallas_call(mix_kernel, name='mix', out_shape=jax.ShapeDtypeStruct((40...  1.66 us

profile of v3, /device:TPU:1, one launch (start us, length us, event | category | flops | bytes accessed | tf_op | source)
XLA Modules:
  0.0 65.6 jit_solution(13886311591641947163)
XLA Ops:
  0.0 0.0 copy-start
  0.0 64.0 %move.1.sums_ref = bf16[1024,512]{1,0:T(8,128)(2,1)S(1)} custom-call(s32[4,3]{1,0:T(4,128)} %pair_hbm.1, s32[1,128]{1,0:T(1,128)} %bitcast.8, bf16[512,128]{1,0:T(8,128)(2,1)} %bitcast.7, bf16[512,1024]{1,0:T(8,128)(2,1)} %coef_ref.1), custom_call_target="tpu_custom_call" | custom-call | tf_op jit(solution)/shard_map/move/pallas_call | solution.py:381
  64.0 0.0 copy-done
  64.0 1.7 %mix.1 = bf16[4096,128]{1,0:T(8,128)(2,1)} custom-call(bf16[4,4]{1,0:T(4,128)(2,1)S(1)} %copy-done, bf16[1024,512]{1,0:T(8,128)(2,1)S(1)} %move.1.sums_ref), custom_call_target="tpu_custom_call" | custom-call | tf_op jit(solution)/shard_map/mix/pallas_call | solution.py:422
Async XLA Ops:
  0.0 64.0 %copy-start = (bf16[4,4]{1,0:T(4,128)(2,1)S(1)}, bf16[4,4]{1,0:T(4,128)(2,1)}, u32[]{:S(2)}) copy-start(bf16[4,4]{1,0:T(4,128)(2,1)} %metric_ref.1) | copy-start | bytes 100

commit v4 on v3

--- a/solution.py
+++ b/solution.py
@@ -184,7 +184,7 @@
     step(1, 0)
     meet(2, 2)
     step(1, 1)
-    coef_out(4, 5)
+    coef_out(4)
 
     kid = (lax.broadcasted_iota(I32, (256, BS), 0) // 2) % SLOTS
     kmask = [jnp.where(kid == k, 1.0, 0.0).astype(BF) for k in range(SLOTS)]
@@ -289,12 +289,13 @@
     coef_aux(0)
     step(2, 0)
     step(2, 1)
-    coef_out(6, 7, 8)
+    coef_out(5, 6)
     coef_aux(1)
     coef_aux(2)
     compute(0)
     step(3, 0)
     step(3, 1)
+    coef_out(7, 8)
     coef_aux(3)
     compute(1)
     compute(2)

time: 65.8 us -> 64.9 us (0.986)
  Pallas kernels: 65.6 us -> 64.8 us
    pallas_call x1, Pallas kernels: 64 us -> 63.1 us  [per_device(): pl.pallas_call(move_kernel, name='move', out_shape=jax.ShapeDtypeStruct((...]
where the time goes in v4:
time: 64.9 us; the launch traced here: 64.8 us
  Pallas kernels  64.8 us (100%)
    pallas_call x1, Pallas kernels, per_device(): pl.pallas_call(move_kernel, name='move', out_shape=jax.ShapeDtypeStruct((...  63.1 us
    pallas_call x1, Pallas kernels, per_device(): pl.pallas_call(mix_kernel, name='mix', out_shape=jax.ShapeDtypeStruct((40...  1.66 us

profile of v4, /device:TPU:1, one launch (start us, length us, event | category | flops | bytes accessed | tf_op | source)
XLA Modules:
  0.0 64.8 jit_solution(18088340763657512921)
XLA Ops:
  0.0 0.0 copy-start
  0.0 63.1 %move.1.sums_ref = bf16[1024,512]{1,0:T(8,128)(2,1)S(1)} custom-call(s32[4,3]{1,0:T(4,128)} %pair_hbm.1, s32[1,128]{1,0:T(1,128)} %bitcast.8, bf16[512,128]{1,0:T(8,128)(2,1)} %bitcast.7, bf16[512,1024]{1,0:T(8,128)(2,1)} %coef_ref.1), custom_call_target="tpu_custom_call" | custom-call | tf_op jit(solution)/shard_map/move/pallas_call | solution.py:382
  63.1 0.0 copy-done
  63.1 1.7 %mix.1 = bf16[4096,128]{1,0:T(8,128)(2,1)} custom-call(bf16[4,4]{1,0:T(4,128)(2,1)S(1)} %copy-done, bf16[1024,512]{1,0:T(8,128)(2,1)S(1)} %move.1.sums_ref), custom_call_target="tpu_custom_call" | custom-call | tf_op jit(solution)/shard_map/mix/pallas_call | solution.py:423
Async XLA Ops:
  0.0 63.1 %copy-start = (bf16[4,4]{1,0:T(4,128)(2,1)S(1)}, bf16[4,4]{1,0:T(4,128)(2,1)}, u32[]{:S(2)}) copy-start(bf16[4,4]{1,0:T(4,128)(2,1)} %metric_ref.1) | copy-start | bytes 100
